TPU v7x, 32 devices: a whole 2x2x4 slice. The times are simulated.
32 devices in a mesh: row: 8 (over y, x, core), col: 4 (over z).
Axes of the slice: x: 2, y: 2, z: 4, core: 2. Of those that a mesh axis runs over, the one named last changes fastest.
Arguments:
- pair: bfloat16 [384, 384, 128], P('row', 'col'), may hold values from -6 to 6
- token_mask: int32 [384], replicated, may hold values from 0 to 1, as said below
- gain: float32 [2, 128], replicated, may hold values from 0.25 to 1.75
- w_proj: bfloat16 [2, 128, 512], replicated, may hold values from -3 to 3
- w_bias: bfloat16 [2, 128, 4], replicated, may hold values from -0.5 to 0.5
- w_out: bfloat16 [2, 128, 128], replicated, may hold values from -0.5 to 0.5
Outputs:
- updated: bfloat16 [384, 384, 128], P('row', 'col')
Inputs may be any that keep to these rules, and one draw needn't show every extreme that they name: `token_mask`: the tokens form 4 chains of 96 positions each; in each chain the first L positions are 1 and the rest 0, with 48 <= L < 96.
All inputs are finite; a program needn't handle non-finite values.
Results may differ from a plain program's by a relative error of at most 0.03.
The roundings to bfloat16 on the way count: a program that leaves them out, or rounds other values in their place, can miss the bound.
Values may be sent and summed in bfloat16 or wider, within the bound.
A program may use at most 128 MiB of HBM per device.

v0:
```python
import math
import jax
import jax.numpy as jnp
from jax import lax
from jax.sharding import PartitionSpec as P

HEADS = 4
HEAD_DIM = 32


def normalize(tile, gain):
    values = tile.astype(jnp.float32)
    average = jnp.mean(values, axis=-1, keepdims=True)
    centred = values - average
    variance = jnp.mean(centred * centred, axis=-1, keepdims=True)
    return (centred * lax.rsqrt(variance + 1e-05) * gain).astype(jnp.bfloat16)


def project(normed, w_proj, w_bias):
    row_count, col_count, channels = normed.shape
    inner = HEADS * HEAD_DIM
    flattened = normed.reshape(row_count * col_count, channels)
    projected = jnp.dot(flattened, w_proj, preferred_element_type=jnp.float32)
    queries = (projected[:, :inner] / jnp.sqrt(jnp.float32(HEAD_DIM))).astype(jnp.bfloat16)
    queries = queries.reshape(row_count, col_count, HEADS, HEAD_DIM)
    key_part = (
        projected[:, inner : 2 * inner].astype(jnp.bfloat16).reshape(row_count, col_count, inner)
    )
    value_part = (
        projected[:, 2 * inner : 3 * inner]
        .astype(jnp.bfloat16)
        .reshape(row_count, col_count, inner)
    )
    gate_part = jax.nn.sigmoid(projected[:, 3 * inner :])
    bias_part = jnp.dot(flattened, w_bias, preferred_element_type=jnp.float32).astype(jnp.bfloat16)
    return (
        queries,
        key_part,
        value_part,
        gate_part,
        bias_part.reshape(row_count, col_count, HEADS),
    )


def keys_from_pairs(normed_piece, w_proj):
    inner = HEADS * HEAD_DIM
    lead = normed_piece.shape[:2]
    flattened = normed_piece.reshape(lead[0] * lead[1], normed_piece.shape[2])
    projected = jnp.dot(flattened, w_proj[:, inner : 3 * inner], preferred_element_type=jnp.float32)
    key_piece = projected[:, :inner].astype(jnp.bfloat16).reshape(lead + (inner,))
    value_piece = projected[:, inner:].astype(jnp.bfloat16).reshape(lead + (inner,))
    return (key_piece, value_piece)


def accumulate(carried, scores, value_piece, form):
    running_max, running_sum, running_acc = carried
    new_max = jnp.maximum(running_max, jnp.max(scores, axis=-1))
    factor = jnp.exp(running_max - new_max)
    weights = jnp.exp(scores - new_max[..., None])
    running_sum = running_sum * factor + jnp.sum(weights, axis=-1)
    product = jnp.einsum(
        form, weights.astype(jnp.bfloat16), value_piece, preferred_element_type=jnp.float32
    )
    return (new_max, running_sum, running_acc * factor[..., None] + product)


def attend_ending(carried, key_piece, value_piece, offset, queries, bias_end, token_mask):
    count = key_piece.shape[0]
    col_count = queries.shape[1]
    key_four = key_piece.reshape(count, col_count, HEADS, HEAD_DIM)
    value_four = value_piece.reshape(count, col_count, HEADS, HEAD_DIM)
    scores = jnp.einsum("ijhd,kjhd->ijhk", queries, key_four, preferred_element_type=jnp.float32)
    bias_slice = lax.dynamic_slice_in_dim(bias_end, offset, count, 0)
    scores = scores + jnp.transpose(bias_slice, (1, 2, 0)).astype(jnp.float32)[:, None]
    live = lax.dynamic_slice_in_dim(token_mask, offset, count, 0)
    scores = jnp.where(live > 0, scores, -1000000000.0)
    return accumulate(carried, scores, value_four, "ijhk,kjhd->ijhd")


def attend_starting(carried, key_piece, value_piece, offset, queries, bias_start, token_mask):
    count = key_piece.shape[1]
    row_count = queries.shape[0]
    key_four = key_piece.reshape(row_count, count, HEADS, HEAD_DIM)
    value_four = value_piece.reshape(row_count, count, HEADS, HEAD_DIM)
    scores = jnp.einsum("ijhd,ikhd->ijhk", queries, key_four, preferred_element_type=jnp.float32)
    bias_slice = lax.dynamic_slice_in_dim(bias_start, offset, count, 1)
    scores = scores + jnp.transpose(bias_slice, (0, 2, 1)).astype(jnp.float32)[None]
    live = lax.dynamic_slice_in_dim(token_mask, offset, count, 0)
    scores = jnp.where(live > 0, scores, -1000000000.0)
    return accumulate(carried, scores, value_four, "ijhk,ikhd->ijhd")


def fold_blocks(carried, pieces, along, convert, attend):
    count = pieces[0].shape[along]
    width = math.gcd(count, 128)

    def one_block(index, carry):
        start = index * width
        blocks = tuple((lax.dynamic_slice_in_dim(piece, start, width, along) for piece in pieces))
        key_block, value_block = convert(blocks)
        return attend(carry, key_block, value_block, start)

    return lax.fori_loop(0, count // width, one_block, carried)


def select_bias(bias_part, row_count, col_count, ending):
    bias_rowwise = lax.all_gather(bias_part, "row", axis=0, tiled=True)
    full_bias = lax.all_gather(bias_rowwise, "col", axis=1, tiled=True)
    if ending:
        return lax.dynamic_slice_in_dim(full_bias, lax.axis_index("row") * row_count, row_count, 1)
    return lax.dynamic_slice_in_dim(full_bias, lax.axis_index("col") * col_count, col_count, 0)


def run_pass(tile, token_mask, gain, w_proj, w_bias, w_out, ending):
    row_count, col_count, channels = tile.shape
    normed = normalize(tile, gain)
    queries, key_part, value_part, gate_part, bias_part = project(normed, w_proj, w_bias)
    bias_local = select_bias(bias_part, row_count, col_count, ending)
    start_max = jnp.full((row_count, col_count, HEADS), -1e30, jnp.float32)
    start_sum = jnp.zeros((row_count, col_count, HEADS), jnp.float32)
    start_acc = jnp.zeros((row_count, col_count, HEADS, HEAD_DIM), jnp.float32)
    initial = (start_max, start_sum, start_acc)

    def project_pairs(blocks):
        return keys_from_pairs(blocks[0], w_proj)

    if ending:

        def ending_step(carry, key_block, value_block, position):
            return attend_ending(
                carry, key_block, value_block, position, queries, bias_local, token_mask
            )

        def fold_pairs(carried, received, offset):
            return fold_blocks(carried, (received,), 0, project_pairs, ending_step)

        result = fold_pairs(
            initial, lax.all_gather(normed, "row", axis=0, tiled=True), jnp.int32(0)
        )
    else:

        def starting_step(carry, key_block, value_block, position):
            return attend_starting(
                carry, key_block, value_block, position, queries, bias_local, token_mask
            )

        def fold_pairs(carried, received, offset):
            return fold_blocks(carried, (received,), 1, project_pairs, starting_step)

        result = fold_pairs(
            initial, lax.all_gather(normed, "col", axis=1, tiled=True), jnp.int32(0)
        )
    final_max, final_sum, final_acc = result
    attended = final_acc / final_sum[..., None]
    gated = (gate_part * attended.reshape(row_count * col_count, HEADS * HEAD_DIM)).astype(
        jnp.bfloat16
    )
    update = jnp.dot(gated, w_out, preferred_element_type=jnp.float32)
    return (tile.astype(jnp.float32) + update.reshape(row_count, col_count, channels)).astype(
        jnp.bfloat16
    )


def local(pair, token_mask, gain, w_proj, w_bias, w_out):
    first = run_pass(pair, token_mask, gain[0], w_proj[0], w_bias[0], w_out[0], True)
    return run_pass(first, token_mask, gain[1], w_proj[1], w_bias[1], w_out[1], False)


def solution(mesh):
    return jax.shard_map(
        local,
        mesh=mesh,
        in_specs=(P("row", "col", None), P(), P(), P(), P(), P()),
        out_specs=P("row", "col", None),
        check_vma=False,
    )
```

profile of v0, /device:TPU:0, one launch (start us, length us, event | category | flops | bytes accessed | tf_op | source)
XLA Modules:
  0.0 606.3 jit_solution(17036669407147317621)
XLA Ops:
  8.4 2.7 fusion.40
  13.7 11.1 %all_gather.19 = bf16[384,96,4]{1,2,0:T(4,128)(2,1)S(1)} all-gather(bf16[48,96,4]{1,2,0:T(4,128)(2,1)S(1)} %copy.62), channel_id=1, replica_groups=mesh['row'=8,'col'=4] {'row'}, dimensions={0}, use_global_device_ids=true | all-gather | bytes 331776 | tf_op jit(solution)/shard_map/all_gather | solution.py:107
  26.6 2.7 fusion.65
  29.3 3.7 copy-done.3
  35.4 5.2 copy.64
  41.4 15.1 %all-gather.7.cloned.1.call-done = bf16[384,384,4]{0,2,1:T(4,128)(2,1)} async-done(((bf16[384,96,4]{0,2,1:T(4,128)(2,1)}), bf16[384,384,4]{0,2,1:T(4,128)(2,1)}) %all-gather.7.cloned.1.call-update) | async-done | bytes 1179664 | tf_op jit(solution)/shard_map/all_gather | solution.py:108
  58.1 58.2 %all-gather.5.cloned.1.call-done = bf16[384,96,128]{2,1,0:T(8,128)(2,1)} async-done(((bf16[48,96,128]{2,1,0:T(8,128)(2,1)}), bf16[384,96,128]{2,1,0:T(8,128)(2,1)}) %all-gather.5.cloned.1.call-update) | async-done | bytes 9437200 | tf_op jit(solution)/shard_map/all_gather | solution.py:138
  116.3 207.9 %while.36 = (s32[]{:T(128)}, f32[48,96,4]{0,2,1:T(4,128)}, f32[48,96,4]{0,2,1:T(4,128)}, f32[48,96,4,32]{0,3,2,1:T(8,128)}, s32[384]{0:T(512)S(1)}, /*index=5*/b...) while((s32[]{:T(128)}, f32[48,96,4]{0,2,1:T(4,128)}, ...), condition=%wide.region_5.6_spmd.clone, body=%wide.region_2.5_spmd.clone.sunk | while | flops 1138280576 | bytes 109233432 | solution.py:103
  116.8 2.1 constant_dynamic-slice_fusion.9
  118.9 2.6 convolution_convert_fusion.6
  121.5 3.0 fusion.106
  124.5 3.2 copy.97
  127.7 5.2 reshape.122
  132.9 6.1 %copy.98 = bf16[128,96,4,32]{0,3,2,1:T(8,128)(2,1)S(1)} copy(bf16[128,96,4,32]{1,0,3,2:T(8,128)(2,1)} %reshape.122) | data formatting | bytes 6291456 | tf_op jit(solution)/shard_map/while/body/eval_jaxpr/reshape;while/body/eval_jaxpr/reshape | solution.py:70
  139.9 10.1 %fusion.107 = (f32[48,96,4]{0,2,1:T(4,128)}, f32[96,4,128,48]{2,3,1,0:T(8,128)}) fusion(f32[48,4,128]{2,0,1:T(8,128)S(1)} %convert_bitcast_fusion.4, pred[128]{0:T(512)(128)(4,1)S(1)} %dynamic-slice_compare_fusion.4, bf16[128,96,4,32]{0,3,2,1:T(8,128)(2,1)S(1)} %copy.98, bf16[48,96,4,32]{0,3,2,1:T(8,128)(2,1)} %get-tuple-element.672), kind=kOutput, calls=%fused_computation.6.clone.1 | convolution fusion | flops 158054400 | bytes 13934720 | tf_op jit(solution)/shard_map/while/body/eval_jaxpr/ijhd,kjhd->ijhk/dot_general | solution.py:72
  151.1 8.3 %fusion.108 = f32[48,96,4]{0,2,1:T(4,128)S(1)} fusion(f32[96,4,128,48]{2,3,1,0:T(8,128)} %get-tuple-element.620, f32[48,96,4]{0,2,1:T(4,128)S(1)} %select_maximum_fusion.4, f32[48,4,128]{2,0,1:T(8,128)S(1)} %convert_bitcast_fusion.4, pred[128]{0:T(512)(128)(4,1)S(1)} %dynamic-slice_compare_fusion.4), kind=kLoop, calls=%fused_computation.5.clone.1 | loop fusion | flops 9418752 | bytes 9683072 | tf_op jit(solution)/shard_map/while/body/eval_jaxpr/reduce_sum | solution.py:60
  161.0 3.2 copy.99
  164.2 5.2 reshape.123
  169.4 6.1 %copy.100 = bf16[128,96,4,32]{0,3,2,1:T(8,128)(2,1)S(1)} copy(bf16[128,96,4,32]{1,0,3,2:T(8,128)(2,1)} %reshape.123) | data formatting | bytes 6291456 | tf_op jit(solution)/shard_map/while/body/eval_jaxpr/reshape;while/body/eval_jaxpr/reshape | solution.py:71
  175.5 8.7 %bitcast_add_fusion.6 = f32[48,96,4,32]{0,3,2,1:T(8,128)} fusion(f32[48,96,4,32]{0,3,2,1:T(8,128)} %get-tuple-element.655, f32[48,96,4]{0,2,1:T(4,128)} %get-tuple-element.622, pred[]{:T(512)S(6)} %compare.6, bf16[128,96,4,32]{0,3,2,1:T(8,128)(2,1)S(1)} %copy.100, f32[96,4,128,48]{2,3,1,0:T(8,128)} %get-tuple-element.620, ...), kind=kOutput, calls=%fused_computation.7.clone.1 | convolution fusion | flops 162201600 | bytes 17547392 | tf_op jit(solution)/shard_map/while/body/eval_jaxpr/ijhk,kjhd->ijhd/dot_general | solution.py:61
  187.0 2.6 convolution_convert_fusion.6
  189.6 3.0 fusion.106
  192.6 3.2 copy.97
  195.8 5.2 reshape.122
  201.0 6.1 %copy.98 = bf16[128,96,4,32]{0,3,2,1:T(8,128)(2,1)S(1)} copy(bf16[128,96,4,32]{1,0,3,2:T(8,128)(2,1)} %reshape.122) | data formatting | bytes 6291456 | tf_op jit(solution)/shard_map/while/body/eval_jaxpr/reshape;while/body/eval_jaxpr/reshape | solution.py:70
  208.0 10.1 %fusion.107 = (f32[48,96,4]{0,2,1:T(4,128)}, f32[96,4,128,48]{2,3,1,0:T(8,128)}) fusion(f32[48,4,128]{2,0,1:T(8,128)S(1)} %convert_bitcast_fusion.4, pred[128]{0:T(512)(128)(4,1)S(1)} %dynamic-slice_compare_fusion.4, bf16[128,96,4,32]{0,3,2,1:T(8,128)(2,1)S(1)} %copy.98, bf16[48,96,4,32]{0,3,2,1:T(8,128)(2,1)} %get-tuple-element.672), kind=kOutput, calls=%fused_computation.6.clone.1 | convolution fusion | flops 158054400 | bytes 13934720 | tf_op jit(solution)/shard_map/while/body/eval_jaxpr/ijhd,kjhd->ijhk/dot_general | solution.py:72
  219.3 8.3 %fusion.108 = f32[48,96,4]{0,2,1:T(4,128)S(1)} fusion(f32[96,4,128,48]{2,3,1,0:T(8,128)} %get-tuple-element.620, f32[48,96,4]{0,2,1:T(4,128)S(1)} %select_maximum_fusion.4, f32[48,4,128]{2,0,1:T(8,128)S(1)} %convert_bitcast_fusion.4, pred[128]{0:T(512)(128)(4,1)S(1)} %dynamic-slice_compare_fusion.4), kind=kLoop, calls=%fused_computation.5.clone.1 | loop fusion | flops 9418752 | bytes 9683072 | tf_op jit(solution)/shard_map/while/body/eval_jaxpr/reduce_sum | solution.py:60
  229.2 3.2 copy.99
  232.4 5.2 reshape.123
  237.6 6.1 %copy.100 = bf16[128,96,4,32]{0,3,2,1:T(8,128)(2,1)S(1)} copy(bf16[128,96,4,32]{1,0,3,2:T(8,128)(2,1)} %reshape.123) | data formatting | bytes 6291456 | tf_op jit(solution)/shard_map/while/body/eval_jaxpr/reshape;while/body/eval_jaxpr/reshape | solution.py:71
  243.7 10.1 %bitcast_add_fusion.6 = f32[48,96,4,32]{0,3,2,1:T(8,128)} fusion(f32[48,96,4,32]{0,3,2,1:T(8,128)} %get-tuple-element.655, f32[48,96,4]{0,2,1:T(4,128)} %get-tuple-element.622, pred[]{:T(512)S(6)} %compare.6, bf16[128,96,4,32]{0,3,2,1:T(8,128)(2,1)S(1)} %copy.100, f32[96,4,128,48]{2,3,1,0:T(8,128)} %get-tuple-element.620, ...), kind=kOutput, calls=%fused_computation.7.clone.1 | convolution fusion | flops 162201600 | bytes 17547392 | tf_op jit(solution)/shard_map/while/body/eval_jaxpr/ijhk,kjhd->ijhd/dot_general | solution.py:61
  256.6 2.6 convolution_convert_fusion.6
  259.2 3.0 fusion.106
  262.3 3.2 copy.97
  265.4 5.2 reshape.122
  270.6 6.1 %copy.98 = bf16[128,96,4,32]{0,3,2,1:T(8,128)(2,1)S(1)} copy(bf16[128,96,4,32]{1,0,3,2:T(8,128)(2,1)} %reshape.122) | data formatting | bytes 6291456 | tf_op jit(solution)/shard_map/while/body/eval_jaxpr/reshape;while/body/eval_jaxpr/reshape | solution.py:70
  277.6 10.1 %fusion.107 = (f32[48,96,4]{0,2,1:T(4,128)}, f32[96,4,128,48]{2,3,1,0:T(8,128)}) fusion(f32[48,4,128]{2,0,1:T(8,128)S(1)} %convert_bitcast_fusion.4, pred[128]{0:T(512)(128)(4,1)S(1)} %dynamic-slice_compare_fusion.4, bf16[128,96,4,32]{0,3,2,1:T(8,128)(2,1)S(1)} %copy.98, bf16[48,96,4,32]{0,3,2,1:T(8,128)(2,1)} %get-tuple-element.672), kind=kOutput, calls=%fused_computation.6.clone.1 | convolution fusion | flops 158054400 | bytes 13934720 | tf_op jit(solution)/shard_map/while/body/eval_jaxpr/ijhd,kjhd->ijhk/dot_general | solution.py:72
  288.9 8.3 %fusion.108 = f32[48,96,4]{0,2,1:T(4,128)S(1)} fusion(f32[96,4,128,48]{2,3,1,0:T(8,128)} %get-tuple-element.620, f32[48,96,4]{0,2,1:T(4,128)S(1)} %select_maximum_fusion.4, f32[48,4,128]{2,0,1:T(8,128)S(1)} %convert_bitcast_fusion.4, pred[128]{0:T(512)(128)(4,1)S(1)} %dynamic-slice_compare_fusion.4), kind=kLoop, calls=%fused_computation.5.clone.1 | loop fusion | flops 9418752 | bytes 9683072 | tf_op jit(solution)/shard_map/while/body/eval_jaxpr/reduce_sum | solution.py:60
  298.8 3.2 copy.99
  302.0 5.2 reshape.123
  307.2 6.1 %copy.100 = bf16[128,96,4,32]{0,3,2,1:T(8,128)(2,1)S(1)} copy(bf16[128,96,4,32]{1,0,3,2:T(8,128)(2,1)} %reshape.123) | data formatting | bytes 6291456 | tf_op jit(solution)/shard_map/while/body/eval_jaxpr/reshape;while/body/eval_jaxpr/reshape | solution.py:71
  313.3 10.1 %bitcast_add_fusion.6 = f32[48,96,4,32]{0,3,2,1:T(8,128)} fusion(f32[48,96,4,32]{0,3,2,1:T(8,128)} %get-tuple-element.655, f32[48,96,4]{0,2,1:T(4,128)} %get-tuple-element.622, pred[]{:T(512)S(6)} %compare.6, bf16[128,96,4,32]{0,3,2,1:T(8,128)(2,1)S(1)} %copy.100, f32[96,4,128,48]{2,3,1,0:T(8,128)} %get-tuple-element.620, ...), kind=kOutput, calls=%fused_computation.7.clone.1 | convolution fusion | flops 162201600 | bytes 17547392 | tf_op jit(solution)/shard_map/while/body/eval_jaxpr/ijhk,kjhd->ijhd/dot_general | solution.py:61
  324.2 6.9 %broadcast_divide_fusion = f32[48,96,4,32]{0,3,2,1:T(8,128)} fusion(f32[48,96,4,32]{0,3,2,1:T(8,128)} %get-tuple-element.315, f32[48,96,4]{0,2,1:T(4,128)} %get-tuple-element.316), kind=kLoop, calls=%fused_computation.58 | loop fusion | flops 589824 | bytes 4792320 | tf_op jit(solution)/shard_map/div | solution.py:154
  331.1 5.4 copy.66
  336.6 2.6 reshape.107
  341.2 2.4 fusion.55
  348.5 9.5 %all_gather.22 = bf16[384,96,4]{1,2,0:T(4,128)(2,1)S(1)} all-gather(bf16[48,96,4]{1,2,0:T(4,128)(2,1)S(1)} %copy.69), channel_id=1, replica_groups=mesh['row'=8,'col'=4] {'row'}, dimensions={0}, use_global_device_ids=true | all-gather | bytes 331776 | tf_op jit(solution)/shard_map/all_gather | solution.py:107
  359.7 2.6 fusion.66
  362.3 3.7 copy-done.4
  370.3 19.2 %all-gather.11.cloned.1.call-done = bf16[384,384,4]{0,2,1:T(4,128)(2,1)} async-done(((bf16[384,96,4]{0,2,1:T(4,128)(2,1)}), bf16[384,384,4]{0,2,1:T(4,128)(2,1)}) %all-gather.11.cloned.1.call-update) | async-done | bytes 1179664 | tf_op jit(solution)/shard_map/all_gather | solution.py:108
  391.9 87.7 %all-gather.9.cloned.1.call-done = bf16[48,384,128]{2,1,0:T(8,128)(2,1)} async-done(((bf16[48,96,128]{2,1,0:T(8,128)(2,1)}), bf16[48,384,128]{2,1,0:T(8,128)(2,1)}) %all-gather.9.cloned.1.call-update) | async-done | bytes 4718608 | tf_op jit(solution)/shard_map/all_gather | solution.py:151
  479.5 107.2 %while.37 = (s32[]{:T(128)}, f32[48,96,4]{1,2,0:T(4,128)S(1)}, f32[48,96,4]{1,2,0:T(4,128)}, f32[48,96,4,32]{1,3,2,0:T(8,128)}, s32[384]{0:T(512)S(1)}, /*index=...) while((s32[]{:T(128)}, f32[48,96,4]{1,2,0:T(4,128)S(1)}, ...), condition=%wide.region_11.12_spmd.clone, body=%wide.region_8.11_spmd.clone.sunk | while | flops 734079104 | bytes 90703208 | solution.py:103
  487.4 5.4 fusion.116
  492.9 8.7 %fusion.117 = f32[48,96,4]{1,2,0:T(4,128)S(1)} fusion(f32[48,4,128,96]{2,3,1,0:T(8,128)} %get-tuple-element.635, f32[48,96,4]{1,2,0:T(4,128)S(1)} %select_maximum_fusion.5, f32[96,4,128]{2,0,1:T(8,128)S(1)} %convert_bitcast_fusion.5, pred[128]{0:T(512)(128)(4,1)S(1)} %dynamic-slice_compare_fusion.5), kind=kLoop, calls=%fused_computation.28.clone.1 | loop fusion | flops 9418752 | bytes 9781376 | tf_op jit(solution)/shard_map/while/body/eval_jaxpr/reduce_sum | solution.py:60
  505.0 8.0 %bitcast_add_fusion.7 = f32[48,96,4,32]{1,3,2,0:T(8,128)S(1)} fusion(f32[48,96,4,32]{1,3,2,0:T(8,128)S(1)} %copy-done, f32[48,4,128,96]{2,3,1,0:T(8,128)} %get-tuple-element.635, f32[48,96,4]{1,2,0:T(4,128)S(1)} %select_maximum_fusion.5, f32[96,4,128]{2,0,1:T(8,128)S(1)} %convert_bitcast_fusion.5, ...), kind=kOutput, calls=%fused_computation.36.clone.1 | convolution fusion | flops 162201600 | bytes 16072833 | tf_op jit(solution)/shard_map/while/body/eval_jaxpr/ijhk,ikhd->ijhd/dot_general | solution.py:61
  522.6 5.4 fusion.116
  528.0 8.7 %fusion.117 = f32[48,96,4]{1,2,0:T(4,128)S(1)} fusion(f32[48,4,128,96]{2,3,1,0:T(8,128)} %get-tuple-element.635, f32[48,96,4]{1,2,0:T(4,128)S(1)} %select_maximum_fusion.5, f32[96,4,128]{2,0,1:T(8,128)S(1)} %convert_bitcast_fusion.5, pred[128]{0:T(512)(128)(4,1)S(1)} %dynamic-slice_compare_fusion.5), kind=kLoop, calls=%fused_computation.28.clone.1 | loop fusion | flops 9418752 | bytes 9781376 | tf_op jit(solution)/shard_map/while/body/eval_jaxpr/reduce_sum | solution.py:60
  541.0 8.0 %bitcast_add_fusion.7 = f32[48,96,4,32]{1,3,2,0:T(8,128)S(1)} fusion(f32[48,96,4,32]{1,3,2,0:T(8,128)S(1)} %copy-done, f32[48,4,128,96]{2,3,1,0:T(8,128)} %get-tuple-element.635, f32[48,96,4]{1,2,0:T(4,128)S(1)} %select_maximum_fusion.5, f32[96,4,128]{2,0,1:T(8,128)S(1)} %convert_bitcast_fusion.5, ...), kind=kOutput, calls=%fused_computation.36.clone.1 | convolution fusion | flops 162201600 | bytes 16072833 | tf_op jit(solution)/shard_map/while/body/eval_jaxpr/ijhk,ikhd->ijhd/dot_general | solution.py:61
  558.6 5.4 fusion.116
  564.1 8.7 %fusion.117 = f32[48,96,4]{1,2,0:T(4,128)S(1)} fusion(f32[48,4,128,96]{2,3,1,0:T(8,128)} %get-tuple-element.635, f32[48,96,4]{1,2,0:T(4,128)S(1)} %select_maximum_fusion.5, f32[96,4,128]{2,0,1:T(8,128)S(1)} %convert_bitcast_fusion.5, pred[128]{0:T(512)(128)(4,1)S(1)} %dynamic-slice_compare_fusion.5), kind=kLoop, calls=%fused_computation.28.clone.1 | loop fusion | flops 9418752 | bytes 9781376 | tf_op jit(solution)/shard_map/while/body/eval_jaxpr/reduce_sum | solution.py:60
  577.1 8.0 %bitcast_add_fusion.7 = f32[48,96,4,32]{1,3,2,0:T(8,128)S(1)} fusion(f32[48,96,4,32]{1,3,2,0:T(8,128)S(1)} %copy-done, f32[48,4,128,96]{2,3,1,0:T(8,128)} %get-tuple-element.635, f32[48,96,4]{1,2,0:T(4,128)S(1)} %select_maximum_fusion.5, f32[96,4,128]{2,0,1:T(8,128)S(1)} %convert_bitcast_fusion.5, ...), kind=kOutput, calls=%fused_computation.36.clone.1 | convolution fusion | flops 162201600 | bytes 16072833 | tf_op jit(solution)/shard_map/while/body/eval_jaxpr/ijhk,ikhd->ijhd/dot_general | solution.py:61
  586.8 2.4 broadcast_divide_fusion.1
  591.0 2.6 reshape.111
  595.7 2.4 fusion.56
  (189 shorter events, 89.0 us)
Async XLA Ops:
  6.5 5.1 copy-start.10
  6.5 4.6 copy-start.24
  6.5 6.6 %copy-start.21 = (bf16[2,128,4]{1,2,0:T(4,128)(2,1)S(1)}, bf16[2,128,4]{1,2,0:T(4,128)(2,1)}, u32[]{:S(2)}) copy-start(bf16[2,128,4]{1,2,0:T(4,128)(2,1)} %param.14) | copy-start | bytes 6148
  6.5 49.9 %all-gather.7.cloned.1.call-start = ((), (), s32[]{:S(2)}) async-start(), calls=%async_computation.1 | async-start | bytes 1474560 | tf_op jit(solution)/shard_map/all_gather | solution.py:108
  13.1 12.7 %copy-start.5 = (bf16[48,96,128]{2,1,0:T(8,128)(2,1)}, bf16[48,96,128]{2,1,0:T(8,128)(2,1)S(1)}, u32[]{:S(2)}) copy-start(bf16[48,96,128]{2,1,0:T(8,128)(2,1)S(1)} %fusion.42) | copy-start | bytes 3538948
  13.1 13.5 %copy-start.17 = (bf16[2,128,512]{2,1,0:T(8,128)(2,1)S(1)}, bf16[2,128,512]{2,1,0:T(8,128)(2,1)}, u32[]{:S(2)}) copy-start(bf16[2,128,512]{2,1,0:T(8,128)(2,1)} %param.13) | copy-start | bytes 786436
  25.8 90.6 %all-gather.5.cloned.1.call-start = ((), (), s32[]{:S(2)}) async-start(), calls=%async_computation | async-start | bytes 10616832 | tf_op jit(solution)/shard_map/all_gather | solution.py:138
  26.5 362.9 %all-gather.11.cloned.1.call-start = ((), (), s32[]{:S(2)}) async-start(), calls=%async_computation.3 | async-start | bytes 1474560 | tf_op jit(solution)/shard_map/all_gather | solution.py:108
  29.3 3.7 copy-start.3
  35.4 80.9 %copy-start.25 = (s32[384]{0:T(512)S(1)}, s32[384]{0:T(512)}, u32[]{:S(2)}) copy-start(s32[384]{0:T(512)} %param.11) | copy-start | bytes 4612
  151.0 8.3 %copy-start.7 = (f32[48,96,4]{0,2,1:T(4,128)S(1)}, f32[48,96,4]{0,2,1:T(4,128)}, u32[]{:S(2)}) copy-start(f32[48,96,4]{0,2,1:T(4,128)} %get-tuple-element.653) | copy-start | bytes 221188 | tf_op jit(solution)/shard_map/while
  151.1 8.3 %copy-start.13 = (f32[48,96,4]{0,2,1:T(4,128)S(1)}, f32[48,96,4]{0,2,1:T(4,128)}, u32[]{:S(2)}) copy-start(f32[48,96,4]{0,2,1:T(4,128)} %get-tuple-element.654) | copy-start | bytes 221188 | tf_op jit(solution)/shard_map/while
  160.3 0.7 copy-start.14
  219.2 8.3 %copy-start.7 = (f32[48,96,4]{0,2,1:T(4,128)S(1)}, f32[48,96,4]{0,2,1:T(4,128)}, u32[]{:S(2)}) copy-start(f32[48,96,4]{0,2,1:T(4,128)} %get-tuple-element.653) | copy-start | bytes 221188 | tf_op jit(solution)/shard_map/while
  219.2 8.3 %copy-start.13 = (f32[48,96,4]{0,2,1:T(4,128)S(1)}, f32[48,96,4]{0,2,1:T(4,128)}, u32[]{:S(2)}) copy-start(f32[48,96,4]{0,2,1:T(4,128)} %get-tuple-element.654) | copy-start | bytes 221188 | tf_op jit(solution)/shard_map/while
  228.5 0.7 copy-start.14
  288.8 8.3 %copy-start.7 = (f32[48,96,4]{0,2,1:T(4,128)S(1)}, f32[48,96,4]{0,2,1:T(4,128)}, u32[]{:S(2)}) copy-start(f32[48,96,4]{0,2,1:T(4,128)} %get-tuple-element.653) | copy-start | bytes 221188 | tf_op jit(solution)/shard_map/while
  288.9 8.3 %copy-start.13 = (f32[48,96,4]{0,2,1:T(4,128)S(1)}, f32[48,96,4]{0,2,1:T(4,128)}, u32[]{:S(2)}) copy-start(f32[48,96,4]{0,2,1:T(4,128)} %get-tuple-element.654) | copy-start | bytes 221188 | tf_op jit(solution)/shard_map/while
  298.1 0.7 copy-start.14
  341.2 2.4 copy-start.11
  341.2 2.4 copy-start.19
  343.7 2.8 copy-start.23
  344.7 1.7 copy-start.8
  344.7 3.2 copy-start.22
  347.9 11.2 %copy-start.6 = (bf16[48,96,128]{2,1,0:T(8,128)(2,1)}, bf16[48,96,128]{2,1,0:T(8,128)(2,1)S(1)}, u32[]{:S(2)}) copy-start(bf16[48,96,128]{2,1,0:T(8,128)(2,1)S(1)} %fusion.39) | copy-start | bytes 3538948
  347.9 11.7 %copy-start.18 = (bf16[2,128,512]{2,1,0:T(8,128)(2,1)S(1)}, bf16[2,128,512]{2,1,0:T(8,128)(2,1)}, u32[]{:S(2)}) copy-start(bf16[2,128,512]{2,1,0:T(8,128)(2,1)} %param.13) | copy-start | bytes 786436
  359.1 120.5 %all-gather.9.cloned.1.call-start = ((), (), s32[]{:S(2)}) async-start(), calls=%async_computation.2 | async-start | bytes 5898240 | tf_op jit(solution)/shard_map/all_gather | solution.py:151
  362.3 3.7 copy-start.4
  479.5 13.3 %copy-start.12 = (f32[48,96,4]{1,2,0:T(4,128)}, f32[48,96,4]{1,2,0:T(4,128)S(1)}, u32[]{:S(2)}) copy-start(f32[48,96,4]{1,2,0:T(4,128)S(1)} %get-tuple-element.692) | copy-start | bytes 221188 | tf_op jit(solution)/shard_map/while
  486.0 1.5 copy-start.2
  492.9 8.7 %copy-start.15 = (f32[48,96,4]{1,2,0:T(4,128)S(1)}, f32[48,96,4]{1,2,0:T(4,128)}, u32[]{:S(2)}) copy-start(f32[48,96,4]{1,2,0:T(4,128)} %get-tuple-element.693) | copy-start | bytes 221188 | tf_op jit(solution)/shard_map/while
  501.8 0.6 copy-start.16
  503.1 1.9 copy-start
  513.0 1.7 copy-start.1
  514.7 13.3 %copy-start.12 = (f32[48,96,4]{1,2,0:T(4,128)}, f32[48,96,4]{1,2,0:T(4,128)S(1)}, u32[]{:S(2)}) copy-start(f32[48,96,4]{1,2,0:T(4,128)S(1)} %get-tuple-element.692) | copy-start | bytes 221188 | tf_op jit(solution)/shard_map/while
  521.1 1.5 copy-start.2
  528.0 8.7 %copy-start.15 = (f32[48,96,4]{1,2,0:T(4,128)S(1)}, f32[48,96,4]{1,2,0:T(4,128)}, u32[]{:S(2)}) copy-start(f32[48,96,4]{1,2,0:T(4,128)} %get-tuple-element.693) | copy-start | bytes 221188 | tf_op jit(solution)/shard_map/while
  537.8 0.6 copy-start.16
  539.2 1.9 copy-start
  549.0 1.7 copy-start.1
  550.7 13.3 %copy-start.12 = (f32[48,96,4]{1,2,0:T(4,128)}, f32[48,96,4]{1,2,0:T(4,128)S(1)}, u32[]{:S(2)}) copy-start(f32[48,96,4]{1,2,0:T(4,128)S(1)} %get-tuple-element.692) | copy-start | bytes 221188 | tf_op jit(solution)/shard_map/while
  557.2 1.5 copy-start.2
  564.1 8.7 %copy-start.15 = (f32[48,96,4]{1,2,0:T(4,128)S(1)}, f32[48,96,4]{1,2,0:T(4,128)}, u32[]{:S(2)}) copy-start(f32[48,96,4]{1,2,0:T(4,128)} %get-tuple-element.693) | copy-start | bytes 221188 | tf_op jit(solution)/shard_map/while
  573.9 0.6 copy-start.16
  575.2 1.9 copy-start
  585.1 1.7 copy-start.1
  595.6 2.4 copy-start.9
  595.6 2.4 copy-start.20
Sparse Core Ops, SparseCore 0:
  25.9 30.5 all-gather.6
  58.4 57.9 all-gather.4
  359.2 30.2 all-gather.10
  390.9 88.6 all-gather.8
where the time goes:
time: 615 us; the launch traced here: 606 us
  local copies, waits for them, and re-layouts  181 us (29%)
  waiting for transfers between devices  181 us (29%)
  matrix products  121 us (20%)
  other arithmetic  86.8 us (14%)
  blocking collectives  20.6 us (3%)
  between operations  13.8 us (2%)
    all_gather x1, waiting for transfers between devices, run_pass(): lax.all_gather(normed, 'col', axis=1, tiled=True)  87.7 us
    all_gather x1, waiting for transfers between devices, run_pass(): lax.all_gather(normed, 'row', axis=0, tiled=True)  58.2 us
    dot_general x6, matrix products, accumulate(): jnp.einsum(form, weights.astype(jnp.bfloat16), value_piece, preferred_ele...  52.8 us
    reduce_sum x6, other arithmetic, accumulate(): running_sum = running_sum * factor + jnp.sum(weights, axis=-1)  51.1 us
    all_gather x2, waiting for transfers between devices, select_bias(): full_bias = lax.all_gather(bias_rowwise, 'col', axis=1, tiled=True)  34.3 us
    reshape x6, local copies, waits for them, and re-layouts, attend_ending(): value_four = value_piece.reshape(count, col_count, HEADS, HEAD_DIM)  33.9 us
    reshape x6, local copies, waits for them, and re-layouts, attend_ending(): key_four = key_piece.reshape(count, col_count, HEADS, HEAD_DIM)  33.8 us
    dot_general x3, matrix products, attend_ending(): jnp.einsum('ijhd,kjhd->ijhk', queries, key_four, preferred_element_type=j...  30.3 us
  transfers between devices with their start and end apart: 4, of which 4 were waited for; matrix products, arithmetic and copies ran while one was open for 4% of the time, Pallas kernels for 0%

commit v1 on v0

--- a/solution.py
+++ b/solution.py
@@ -135,7 +135,11 @@
             return fold_blocks(carried, (received,), 0, project_pairs, ending_step)
 
         result = fold_pairs(
-            initial, lax.all_gather(normed, "row", axis=0, tiled=True), jnp.int32(0)
+            initial,
+            jnp.concatenate(
+                lax.all_to_all(jnp.stack([normed] * lax.axis_size("row")), "row", 0, 0), axis=0
+            ),
+            jnp.int32(0),
         )
     else:
 

time: 615 us -> 666 us (1.083)
  blocking collectives: 20.6 us -> 119 us
  waiting for transfers between devices: 181 us -> 124 us
    all_gather x2, blocking collectives: 20.6 us -> 119 us  [select_bias(): bias_rowwise = lax.all_gather(bias_part, 'row', axis=0, tiled=True)]
    all_gather x1 -> x0, waiting for transfers between devices: 58.2 us -> none  [run_pass(): lax.all_gather(normed, 'row', axis=0, tiled=True)]
    unnamed x37 -> x35, local copies, waits for them, and re-layouts: 15.2 us -> 15.1 us
  transfers between devices with their start and end apart: 4 -> 4, of which waited for: 4 -> 3; matrix products, arithmetic and copies ran while one was open for 4% -> 3% of each run, Pallas kernels for 0% -> 0%
where the time goes in v1:
time: 666 us; the launch traced here: 656 us
  local copies, waits for them, and re-layouts  186 us (28%)
  waiting for transfers between devices  124 us (19%)
  matrix products  120 us (18%)
  blocking collectives  119 us (18%)
  other arithmetic  86.8 us (13%)
  between operations  13.8 us (2%)
    all_gather x2, blocking collectives, select_bias(): bias_rowwise = lax.all_gather(bias_part, 'row', axis=0, tiled=True)  119 us
    all_gather x1, waiting for transfers between devices, run_pass(): lax.all_gather(normed, 'col', axis=1, tiled=True)  87.8 us
    dot_general x6, matrix products, accumulate(): jnp.einsum(form, weights.astype(jnp.bfloat16), value_piece, preferred_ele...  52.8 us
    reduce_sum x6, other arithmetic, accumulate(): running_sum = running_sum * factor + jnp.sum(weights, axis=-1)  51.1 us
    all_gather x2, waiting for transfers between devices, select_bias(): full_bias = lax.all_gather(bias_rowwise, 'col', axis=1, tiled=True)  35.3 us
    reshape x6, local copies, waits for them, and re-layouts, attend_ending(): value_four = value_piece.reshape(count, col_count, HEADS, HEAD_DIM)  33.9 us
    reshape x6, local copies, waits for them, and re-layouts, attend_ending(): key_four = key_piece.reshape(count, col_count, HEADS, HEAD_DIM)  33.8 us
    dot_general x3, matrix products, attend_ending(): jnp.einsum('ijhd,kjhd->ijhk', queries, key_four, preferred_element_type=j...  30.3 us
  transfers between devices with their start and end apart: 4, of which 3 were waited for; matrix products, arithmetic and copies ran while one was open for 3% of the time, Pallas kernels for 0%

profile of v1, /device:TPU:0, one launch (start us, length us, event | category | flops | bytes accessed | tf_op | source)
XLA Modules:
  0.0 656.1 jit_solution(2584492703421960636)
XLA Ops:
  8.4 2.7 fusion.40
  13.2 5.3 stack.2
  18.5 5.3 all-to-all-start
  24.5 109.1 %all_gather.15 = bf16[384,96,4]{1,2,0:T(4,128)(2,1)S(1)} all-gather(bf16[48,96,4]{1,2,0:T(4,128)(2,1)S(1)} %copy.62), channel_id=1, replica_groups=mesh['row'=8,'col'=4] {'row'}, dimensions={0}, use_global_device_ids=true | all-gather | bytes 331776 | tf_op jit(solution)/shard_map/all_gather | solution.py:107
  136.1 3.7 copy-done.3
  142.2 5.2 copy.64
  148.2 17.9 %all-gather.4.cloned.1.call-done = bf16[384,384,4]{0,2,1:T(4,128)(2,1)} async-done(((bf16[384,96,4]{0,2,1:T(4,128)(2,1)}), bf16[384,384,4]{0,2,1:T(4,128)(2,1)}) %all-gather.4.cloned.1.call-update) | async-done | bytes 1179664 | tf_op jit(solution)/shard_map/all_gather | solution.py:108
  167.7 207.9 %while.36 = (s32[]{:T(128)}, f32[48,96,4]{0,2,1:T(4,128)}, f32[48,96,4]{0,2,1:T(4,128)}, f32[48,96,4,32]{0,3,2,1:T(8,128)}, s32[384]{0:T(512)S(1)}, /*index=5*/b...) while((s32[]{:T(128)}, f32[48,96,4]{0,2,1:T(4,128)}, ...), condition=%wide.region_5.6_spmd.clone, body=%wide.region_2.5_spmd.clone.sunk | while | flops 1138280576 | bytes 109233432 | solution.py:103
  168.1 2.1 constant_dynamic-slice_fusion.9
  170.2 2.6 convolution_convert_fusion.6
  172.9 3.0 fusion.106
  175.9 3.2 copy.97
  179.1 5.2 reshape.128
  184.2 6.1 copy.98
  191.3 10.1 %fusion.107 = (f32[48,96,4]{0,2,1:T(4,128)}, f32[96,4,128,48]{2,3,1,0:T(8,128)}) fusion(f32[48,4,128]{2,0,1:T(8,128)S(1)} %convert_bitcast_fusion.4, pred[128]{0:T(512)(128)(4,1)S(1)} %dynamic-slice_compare_fusion.4, bf16[128,96,4,32]{0,3,2,1:T(8,128)(2,1)S(1)} %copy.98, bf16[48,96,4,32]{0,3,2,1:T(8,128)(2,1)} %get-tuple-element.672), kind=kOutput, calls=%fused_computation.6.clone.1 | convolution fusion | flops 158054400 | bytes 13934720 | tf_op jit(solution)/shard_map/while/body/eval_jaxpr/ijhd,kjhd->ijhk/dot_general | solution.py:72
  202.4 8.3 %fusion.108 = f32[48,96,4]{0,2,1:T(4,128)S(1)} fusion(f32[96,4,128,48]{2,3,1,0:T(8,128)} %get-tuple-element.620, f32[48,96,4]{0,2,1:T(4,128)S(1)} %select_maximum_fusion.4, f32[48,4,128]{2,0,1:T(8,128)S(1)} %convert_bitcast_fusion.4, pred[128]{0:T(512)(128)(4,1)S(1)} %dynamic-slice_compare_fusion.4), kind=kLoop, calls=%fused_computation.5.clone.1 | loop fusion | flops 9418752 | bytes 9683072 | tf_op jit(solution)/shard_map/while/body/eval_jaxpr/reduce_sum | solution.py:60
  212.4 3.2 copy.99
  215.6 5.2 reshape.129
  220.8 6.1 copy.100
  226.9 8.7 %bitcast_add_fusion.6 = f32[48,96,4,32]{0,3,2,1:T(8,128)} fusion(f32[48,96,4,32]{0,3,2,1:T(8,128)} %get-tuple-element.655, f32[48,96,4]{0,2,1:T(4,128)} %get-tuple-element.622, pred[]{:T(512)S(6)} %compare.6, bf16[128,96,4,32]{0,3,2,1:T(8,128)(2,1)S(1)} %copy.100, f32[96,4,128,48]{2,3,1,0:T(8,128)} %get-tuple-element.620, ...), kind=kOutput, calls=%fused_computation.7.clone.1 | convolution fusion | flops 162201600 | bytes 17547392 | tf_op jit(solution)/shard_map/while/body/eval_jaxpr/ijhk,kjhd->ijhd/dot_general | solution.py:61
  238.3 2.6 convolution_convert_fusion.6
  241.0 3.0 fusion.106
  244.0 3.2 copy.97
  247.2 5.2 reshape.128
  252.3 6.1 copy.98
  259.4 10.1 %fusion.107 = (f32[48,96,4]{0,2,1:T(4,128)}, f32[96,4,128,48]{2,3,1,0:T(8,128)}) fusion(f32[48,4,128]{2,0,1:T(8,128)S(1)} %convert_bitcast_fusion.4, pred[128]{0:T(512)(128)(4,1)S(1)} %dynamic-slice_compare_fusion.4, bf16[128,96,4,32]{0,3,2,1:T(8,128)(2,1)S(1)} %copy.98, bf16[48,96,4,32]{0,3,2,1:T(8,128)(2,1)} %get-tuple-element.672), kind=kOutput, calls=%fused_computation.6.clone.1 | convolution fusion | flops 158054400 | bytes 13934720 | tf_op jit(solution)/shard_map/while/body/eval_jaxpr/ijhd,kjhd->ijhk/dot_general | solution.py:72
  270.6 8.3 %fusion.108 = f32[48,96,4]{0,2,1:T(4,128)S(1)} fusion(f32[96,4,128,48]{2,3,1,0:T(8,128)} %get-tuple-element.620, f32[48,96,4]{0,2,1:T(4,128)S(1)} %select_maximum_fusion.4, f32[48,4,128]{2,0,1:T(8,128)S(1)} %convert_bitcast_fusion.4, pred[128]{0:T(512)(128)(4,1)S(1)} %dynamic-slice_compare_fusion.4), kind=kLoop, calls=%fused_computation.5.clone.1 | loop fusion | flops 9418752 | bytes 9683072 | tf_op jit(solution)/shard_map/while/body/eval_jaxpr/reduce_sum | solution.py:60
  280.6 3.2 copy.99
  283.8 5.2 reshape.129
  288.9 6.1 copy.100
  295.1 10.1 %bitcast_add_fusion.6 = f32[48,96,4,32]{0,3,2,1:T(8,128)} fusion(f32[48,96,4,32]{0,3,2,1:T(8,128)} %get-tuple-element.655, f32[48,96,4]{0,2,1:T(4,128)} %get-tuple-element.622, pred[]{:T(512)S(6)} %compare.6, bf16[128,96,4,32]{0,3,2,1:T(8,128)(2,1)S(1)} %copy.100, f32[96,4,128,48]{2,3,1,0:T(8,128)} %get-tuple-element.620, ...), kind=kOutput, calls=%fused_computation.7.clone.1 | convolution fusion | flops 162201600 | bytes 17547392 | tf_op jit(solution)/shard_map/while/body/eval_jaxpr/ijhk,kjhd->ijhd/dot_general | solution.py:61
  307.9 2.6 convolution_convert_fusion.6
  310.6 3.0 fusion.106
  313.6 3.2 copy.97
  316.8 5.2 reshape.128
  321.9 6.1 copy.98
  329.0 10.1 %fusion.107 = (f32[48,96,4]{0,2,1:T(4,128)}, f32[96,4,128,48]{2,3,1,0:T(8,128)}) fusion(f32[48,4,128]{2,0,1:T(8,128)S(1)} %convert_bitcast_fusion.4, pred[128]{0:T(512)(128)(4,1)S(1)} %dynamic-slice_compare_fusion.4, bf16[128,96,4,32]{0,3,2,1:T(8,128)(2,1)S(1)} %copy.98, bf16[48,96,4,32]{0,3,2,1:T(8,128)(2,1)} %get-tuple-element.672), kind=kOutput, calls=%fused_computation.6.clone.1 | convolution fusion | flops 158054400 | bytes 13934720 | tf_op jit(solution)/shard_map/while/body/eval_jaxpr/ijhd,kjhd->ijhk/dot_general | solution.py:72
  340.2 8.3 %fusion.108 = f32[48,96,4]{0,2,1:T(4,128)S(1)} fusion(f32[96,4,128,48]{2,3,1,0:T(8,128)} %get-tuple-element.620, f32[48,96,4]{0,2,1:T(4,128)S(1)} %select_maximum_fusion.4, f32[48,4,128]{2,0,1:T(8,128)S(1)} %convert_bitcast_fusion.4, pred[128]{0:T(512)(128)(4,1)S(1)} %dynamic-slice_compare_fusion.4), kind=kLoop, calls=%fused_computation.5.clone.1 | loop fusion | flops 9418752 | bytes 9683072 | tf_op jit(solution)/shard_map/while/body/eval_jaxpr/reduce_sum | solution.py:60
  350.2 3.2 copy.99
  353.4 5.2 reshape.129
  358.6 6.1 copy.100
  364.7 10.1 %bitcast_add_fusion.6 = f32[48,96,4,32]{0,3,2,1:T(8,128)} fusion(f32[48,96,4,32]{0,3,2,1:T(8,128)} %get-tuple-element.655, f32[48,96,4]{0,2,1:T(4,128)} %get-tuple-element.622, pred[]{:T(512)S(6)} %compare.6, bf16[128,96,4,32]{0,3,2,1:T(8,128)(2,1)S(1)} %copy.100, f32[96,4,128,48]{2,3,1,0:T(8,128)} %get-tuple-element.620, ...), kind=kOutput, calls=%fused_computation.7.clone.1 | convolution fusion | flops 162201600 | bytes 17547392 | tf_op jit(solution)/shard_map/while/body/eval_jaxpr/ijhk,kjhd->ijhd/dot_general | solution.py:61
  375.6 6.9 %broadcast_divide_fusion = f32[48,96,4,32]{0,3,2,1:T(8,128)} fusion(f32[48,96,4,32]{0,3,2,1:T(8,128)} %get-tuple-element.315, f32[48,96,4]{0,2,1:T(4,128)} %get-tuple-element.316), kind=kLoop, calls=%fused_computation.58 | loop fusion | flops 589824 | bytes 4792320 | tf_op jit(solution)/shard_map/div | solution.py:158
  382.5 5.4 copy.66
  387.9 2.6 reshape.113
  392.6 2.4 fusion.55
  399.9 9.5 %all_gather.18 = bf16[384,96,4]{1,2,0:T(4,128)(2,1)S(1)} all-gather(bf16[48,96,4]{1,2,0:T(4,128)(2,1)S(1)} %copy.69), channel_id=1, replica_groups=mesh['row'=8,'col'=4] {'row'}, dimensions={0}, use_global_device_ids=true | all-gather | bytes 331776 | tf_op jit(solution)/shard_map/all_gather | solution.py:107
  411.2 2.6 fusion.66
  413.8 3.7 copy-done.4
  421.7 17.4 %all-gather.8.cloned.1.call-done = bf16[384,384,4]{0,2,1:T(4,128)(2,1)} async-done(((bf16[384,96,4]{0,2,1:T(4,128)(2,1)}), bf16[384,384,4]{0,2,1:T(4,128)(2,1)}) %all-gather.8.cloned.1.call-update) | async-done | bytes 1179664 | tf_op jit(solution)/shard_map/all_gather | solution.py:108
  441.5 87.8 %all-gather.6.cloned.1.call-done = bf16[48,384,128]{2,1,0:T(8,128)(2,1)} async-done(((bf16[48,96,128]{2,1,0:T(8,128)(2,1)}), bf16[48,384,128]{2,1,0:T(8,128)(2,1)}) %all-gather.6.cloned.1.call-update) | async-done | bytes 4718608 | tf_op jit(solution)/shard_map/all_gather | solution.py:155
  529.4 107.2 %while.37 = (s32[]{:T(128)}, f32[48,96,4]{1,2,0:T(4,128)S(1)}, f32[48,96,4]{1,2,0:T(4,128)}, f32[48,96,4,32]{1,3,2,0:T(8,128)}, s32[384]{0:T(512)S(1)}, /*index=...) while((s32[]{:T(128)}, f32[48,96,4]{1,2,0:T(4,128)S(1)}, ...), condition=%wide.region_11.12_spmd.clone, body=%wide.region_8.11_spmd.clone.sunk | while | flops 734079104 | bytes 90703208 | solution.py:103
  537.3 5.4 fusion.116
  542.7 8.7 %fusion.117 = f32[48,96,4]{1,2,0:T(4,128)S(1)} fusion(f32[48,4,128,96]{2,3,1,0:T(8,128)} %get-tuple-element.635, f32[48,96,4]{1,2,0:T(4,128)S(1)} %select_maximum_fusion.5, f32[96,4,128]{2,0,1:T(8,128)S(1)} %convert_bitcast_fusion.5, pred[128]{0:T(512)(128)(4,1)S(1)} %dynamic-slice_compare_fusion.5), kind=kLoop, calls=%fused_computation.28.clone.1 | loop fusion | flops 9418752 | bytes 9781376 | tf_op jit(solution)/shard_map/while/body/eval_jaxpr/reduce_sum | solution.py:60
  554.8 8.0 %bitcast_add_fusion.7 = f32[48,96,4,32]{1,3,2,0:T(8,128)S(1)} fusion(f32[48,96,4,32]{1,3,2,0:T(8,128)S(1)} %copy-done, f32[48,4,128,96]{2,3,1,0:T(8,128)} %get-tuple-element.635, f32[48,96,4]{1,2,0:T(4,128)S(1)} %select_maximum_fusion.5, f32[96,4,128]{2,0,1:T(8,128)S(1)} %convert_bitcast_fusion.5, ...), kind=kOutput, calls=%fused_computation.36.clone.1 | convolution fusion | flops 162201600 | bytes 16072833 | tf_op jit(solution)/shard_map/while/body/eval_jaxpr/ijhk,ikhd->ijhd/dot_general | solution.py:61
  572.4 5.4 fusion.116
  577.9 8.7 %fusion.117 = f32[48,96,4]{1,2,0:T(4,128)S(1)} fusion(f32[48,4,128,96]{2,3,1,0:T(8,128)} %get-tuple-element.635, f32[48,96,4]{1,2,0:T(4,128)S(1)} %select_maximum_fusion.5, f32[96,4,128]{2,0,1:T(8,128)S(1)} %convert_bitcast_fusion.5, pred[128]{0:T(512)(128)(4,1)S(1)} %dynamic-slice_compare_fusion.5), kind=kLoop, calls=%fused_computation.28.clone.1 | loop fusion | flops 9418752 | bytes 9781376 | tf_op jit(solution)/shard_map/while/body/eval_jaxpr/reduce_sum | solution.py:60
  590.9 8.0 %bitcast_add_fusion.7 = f32[48,96,4,32]{1,3,2,0:T(8,128)S(1)} fusion(f32[48,96,4,32]{1,3,2,0:T(8,128)S(1)} %copy-done, f32[48,4,128,96]{2,3,1,0:T(8,128)} %get-tuple-element.635, f32[48,96,4]{1,2,0:T(4,128)S(1)} %select_maximum_fusion.5, f32[96,4,128]{2,0,1:T(8,128)S(1)} %convert_bitcast_fusion.5, ...), kind=kOutput, calls=%fused_computation.36.clone.1 | convolution fusion | flops 162201600 | bytes 16072833 | tf_op jit(solution)/shard_map/while/body/eval_jaxpr/ijhk,ikhd->ijhd/dot_general | solution.py:61
  608.4 5.4 fusion.116
  613.9 8.7 %fusion.117 = f32[48,96,4]{1,2,0:T(4,128)S(1)} fusion(f32[48,4,128,96]{2,3,1,0:T(8,128)} %get-tuple-element.635, f32[48,96,4]{1,2,0:T(4,128)S(1)} %select_maximum_fusion.5, f32[96,4,128]{2,0,1:T(8,128)S(1)} %convert_bitcast_fusion.5, pred[128]{0:T(512)(128)(4,1)S(1)} %dynamic-slice_compare_fusion.5), kind=kLoop, calls=%fused_computation.28.clone.1 | loop fusion | flops 9418752 | bytes 9781376 | tf_op jit(solution)/shard_map/while/body/eval_jaxpr/reduce_sum | solution.py:60
  626.9 8.0 %bitcast_add_fusion.7 = f32[48,96,4,32]{1,3,2,0:T(8,128)S(1)} fusion(f32[48,96,4,32]{1,3,2,0:T(8,128)S(1)} %copy-done, f32[48,4,128,96]{2,3,1,0:T(8,128)} %get-tuple-element.635, f32[48,96,4]{1,2,0:T(4,128)S(1)} %select_maximum_fusion.5, f32[96,4,128]{2,0,1:T(8,128)S(1)} %convert_bitcast_fusion.5, ...), kind=kOutput, calls=%fused_computation.36.clone.1 | convolution fusion | flops 162201600 | bytes 16072833 | tf_op jit(solution)/shard_map/while/body/eval_jaxpr/ijhk,ikhd->ijhd/dot_general | solution.py:61
  636.6 2.4 broadcast_divide_fusion.1
  640.8 2.6 reshape.117
  645.5 2.4 fusion.56
  (187 shorter events, 89.8 us)
Async XLA Ops:
  6.5 5.2 copy-start.9
  6.5 4.6 copy-start.23
  18.5 5.4 copy-start.20
  18.5 149.2 %all-to-all-start = ((bf16[8,48,96,128]{3,2,1,0:T(8,128)(2,1)}), bf16[8,48,96,128]{3,2,1,0:T(8,128)(2,1)}, u32[]{:S(2)}, u32[]{:S(2)}) async-start(bf16[8,48,96,128]{3,2,1,0:T(8,128)(2,1)} %stack.2), calls=%async_computation | async-start | bytes 18874368 | tf_op jit(solution)/shard_map/all_to_all | solution.py:140
  23.8 110.9 %copy-start.16 = (bf16[2,128,512]{2,1,0:T(8,128)(2,1)S(1)}, bf16[2,128,512]{2,1,0:T(8,128)(2,1)}, u32[]{:S(2)}) copy-start(bf16[2,128,512]{2,1,0:T(8,128)(2,1)} %param.13) | copy-start | bytes 786436
  23.8 142.2 %all-gather.4.cloned.1.call-start = ((), (), s32[]{:S(2)}) async-start(), calls=%async_computation.1 | async-start | bytes 1474560 | tf_op jit(solution)/shard_map/all_gather | solution.py:108
  134.6 304.5 %all-gather.8.cloned.1.call-start = ((), (), s32[]{:S(2)}) async-start(), calls=%async_computation.3 | async-start | bytes 1474560 | tf_op jit(solution)/shard_map/all_gather | solution.py:108
  136.1 3.7 copy-start.3
  142.2 25.5 %copy-start.24 = (s32[384]{0:T(512)S(1)}, s32[384]{0:T(512)}, u32[]{:S(2)}) copy-start(s32[384]{0:T(512)} %param.11) | copy-start | bytes 4612
  202.4 8.3 %copy-start.6 = (f32[48,96,4]{0,2,1:T(4,128)S(1)}, f32[48,96,4]{0,2,1:T(4,128)}, u32[]{:S(2)}) copy-start(f32[48,96,4]{0,2,1:T(4,128)} %get-tuple-element.653) | copy-start | bytes 221188 | tf_op jit(solution)/shard_map/while
  202.4 8.3 %copy-start.12 = (f32[48,96,4]{0,2,1:T(4,128)S(1)}, f32[48,96,4]{0,2,1:T(4,128)}, u32[]{:S(2)}) copy-start(f32[48,96,4]{0,2,1:T(4,128)} %get-tuple-element.654) | copy-start | bytes 221188 | tf_op jit(solution)/shard_map/while
  211.7 0.7 copy-start.13
  270.6 8.3 %copy-start.6 = (f32[48,96,4]{0,2,1:T(4,128)S(1)}, f32[48,96,4]{0,2,1:T(4,128)}, u32[]{:S(2)}) copy-start(f32[48,96,4]{0,2,1:T(4,128)} %get-tuple-element.653) | copy-start | bytes 221188 | tf_op jit(solution)/shard_map/while
  270.6 8.3 %copy-start.12 = (f32[48,96,4]{0,2,1:T(4,128)S(1)}, f32[48,96,4]{0,2,1:T(4,128)}, u32[]{:S(2)}) copy-start(f32[48,96,4]{0,2,1:T(4,128)} %get-tuple-element.654) | copy-start | bytes 221188 | tf_op jit(solution)/shard_map/while
  279.9 0.7 copy-start.13
  340.2 8.3 %copy-start.6 = (f32[48,96,4]{0,2,1:T(4,128)S(1)}, f32[48,96,4]{0,2,1:T(4,128)}, u32[]{:S(2)}) copy-start(f32[48,96,4]{0,2,1:T(4,128)} %get-tuple-element.653) | copy-start | bytes 221188 | tf_op jit(solution)/shard_map/while
  340.2 8.3 %copy-start.12 = (f32[48,96,4]{0,2,1:T(4,128)S(1)}, f32[48,96,4]{0,2,1:T(4,128)}, u32[]{:S(2)}) copy-start(f32[48,96,4]{0,2,1:T(4,128)} %get-tuple-element.654) | copy-start | bytes 221188 | tf_op jit(solution)/shard_map/while
  349.5 0.7 copy-start.13
  392.6 2.4 copy-start.10
  392.6 2.4 copy-start.18
  395.0 2.8 copy-start.22
  396.1 1.7 copy-start.7
  396.1 3.2 copy-start.21
  399.3 11.2 %copy-start.5 = (bf16[48,96,128]{2,1,0:T(8,128)(2,1)}, bf16[48,96,128]{2,1,0:T(8,128)(2,1)S(1)}, u32[]{:S(2)}) copy-start(bf16[48,96,128]{2,1,0:T(8,128)(2,1)S(1)} %fusion.39) | copy-start | bytes 3538948
  399.3 11.9 %copy-start.17 = (bf16[2,128,512]{2,1,0:T(8,128)(2,1)S(1)}, bf16[2,128,512]{2,1,0:T(8,128)(2,1)}, u32[]{:S(2)}) copy-start(bf16[2,128,512]{2,1,0:T(8,128)(2,1)} %param.13) | copy-start | bytes 786436
  410.4 119.0 %all-gather.6.cloned.1.call-start = ((), (), s32[]{:S(2)}) async-start(), calls=%async_computation.2 | async-start | bytes 5898240 | tf_op jit(solution)/shard_map/all_gather | solution.py:155
  413.8 3.7 copy-start.4
  529.4 13.3 %copy-start.11 = (f32[48,96,4]{1,2,0:T(4,128)}, f32[48,96,4]{1,2,0:T(4,128)S(1)}, u32[]{:S(2)}) copy-start(f32[48,96,4]{1,2,0:T(4,128)S(1)} %get-tuple-element.692) | copy-start | bytes 221188 | tf_op jit(solution)/shard_map/while
  535.8 1.5 copy-start.2
  542.7 8.7 %copy-start.14 = (f32[48,96,4]{1,2,0:T(4,128)S(1)}, f32[48,96,4]{1,2,0:T(4,128)}, u32[]{:S(2)}) copy-start(f32[48,96,4]{1,2,0:T(4,128)} %get-tuple-element.693) | copy-start | bytes 221188 | tf_op jit(solution)/shard_map/while
  551.6 0.6 copy-start.15
  552.9 1.9 copy-start
  562.8 1.7 copy-start.1
  564.5 13.3 %copy-start.11 = (f32[48,96,4]{1,2,0:T(4,128)}, f32[48,96,4]{1,2,0:T(4,128)S(1)}, u32[]{:S(2)}) copy-start(f32[48,96,4]{1,2,0:T(4,128)S(1)} %get-tuple-element.692) | copy-start | bytes 221188 | tf_op jit(solution)/shard_map/while
  570.9 1.5 copy-start.2
  577.8 8.7 %copy-start.14 = (f32[48,96,4]{1,2,0:T(4,128)S(1)}, f32[48,96,4]{1,2,0:T(4,128)}, u32[]{:S(2)}) copy-start(f32[48,96,4]{1,2,0:T(4,128)} %get-tuple-element.693) | copy-start | bytes 221188 | tf_op jit(solution)/shard_map/while
  587.6 0.6 copy-start.15
  589.0 1.9 copy-start
  598.8 1.7 copy-start.1
  600.5 13.3 %copy-start.11 = (f32[48,96,4]{1,2,0:T(4,128)}, f32[48,96,4]{1,2,0:T(4,128)S(1)}, u32[]{:S(2)}) copy-start(f32[48,96,4]{1,2,0:T(4,128)S(1)} %get-tuple-element.692) | copy-start | bytes 221188 | tf_op jit(solution)/shard_map/while
  607.0 1.5 copy-start.2
  613.9 8.7 %copy-start.14 = (f32[48,96,4]{1,2,0:T(4,128)S(1)}, f32[48,96,4]{1,2,0:T(4,128)}, u32[]{:S(2)}) copy-start(f32[48,96,4]{1,2,0:T(4,128)} %get-tuple-element.693) | copy-start | bytes 221188 | tf_op jit(solution)/shard_map/while
  623.7 0.6 copy-start.15
  625.0 1.9 copy-start
  634.9 1.7 copy-start.1
  645.5 2.4 copy-start.8
  645.5 2.4 copy-start.19
Sparse Core Ops, SparseCore 0:
  134.7 31.3 all-gather.3
  410.5 28.5 all-gather.7
  440.7 88.6 all-gather.5
